TPU v7x, 32 devices: a whole 2x2x4 slice. The times are simulated.
32 devices in a mesh: occ: 4 (over z), vir: 8 (over y, x, core).
Axes of the slice: x: 2, y: 2, z: 4, core: 2. Of those that a mesh axis runs over, the one named last changes fastest.
Arguments:
- amplitudes: bfloat16 [40, 40, 400, 400], P('occ', None, 'vir'), may hold values from -6 to 6
- integrals: bfloat16 [400, 400, 3200], P('vir', 'occ'), may hold values from -0.109375 to 0.109375
- batch_index: int32 [1], replicated, may hold values from 0 to 49
- eps_occ: float32 [40], replicated, may hold values from -1 to -0.3
- eps_vir: float32 [400], replicated, may hold values from 0.2 to 1.5
Outputs:
- update: float32 [400, 400, 1600], P(None, 'vir', 'occ')
Inputs may be any that keep to these rules, and one draw needn't show every extreme that they name: Selects the virtual orbitals d from 8 * batch_index to 8 * batch_index + 7.
All inputs are finite; a program needn't handle non-finite values.
Results may differ from a plain program's by a relative error of at most 0.0029.
Values may be sent and summed in bfloat16 or wider, within the bound.
A program may use at most 384 MiB of HBM per device.

v0:
```python
import jax
import jax.numpy as jnp
from jax import lax
from jax.sharding import PartitionSpec as P

NB = 8


def shards(amplitudes, integrals, batch_index, eps_occ, eps_vir):
    occ_rows = amplitudes.shape[0]
    occ_all = amplitudes.shape[1]
    vir_local = amplitudes.shape[2]
    block_a = integrals.shape[0]
    block_b = integrals.shape[1]
    begin = batch_index[0] * NB
    sliced = lax.dynamic_slice_in_dim(amplitudes, begin, NB, 3)
    sliced = sliced.reshape(occ_rows, occ_all, vir_local * NB)
    weights_flat = integrals.reshape(block_a * block_b, integrals.shape[2])
    dims_last = (((1,), (1,)), ((), ()))
    columns = lax.all_gather(sliced, "vir", axis=2, tiled=True)
    columns = columns.reshape(occ_rows * occ_all, columns.shape[2])
    ladder = lax.dot_general(
        weights_flat,
        lax.all_gather(columns, "occ", axis=0, tiled=True),
        dims_last,
        preferred_element_type=jnp.float32,
    )
    ladder = 0.5 * ladder.reshape(block_a, block_b, occ_all, occ_all)
    mixed = (ladder - jnp.transpose(ladder, (0, 1, 3, 2))).astype(jnp.bfloat16)
    mixed = mixed.reshape(block_a, block_b, occ_all * occ_all)
    own_rows = lax.all_to_all(mixed, "occ", split_axis=2, concat_axis=1, tiled=True)
    relaid = lax.all_to_all(own_rows, "vir", split_axis=1, concat_axis=0, tiled=True)
    mirrored = jnp.swapaxes(own_rows, 0, 1)
    pair_count = relaid.shape[2]
    pair_rows = pair_count // occ_all
    width_b = relaid.shape[1]
    occ_index = lax.axis_index("occ")
    vir_index = lax.axis_index("vir")
    energy_rows = lax.dynamic_slice_in_dim(eps_occ, occ_index * pair_rows, pair_rows, 0)
    pair_energy = (energy_rows[:, None] + eps_occ[None, :]).reshape(pair_count)
    energy_cols = lax.dynamic_slice_in_dim(eps_vir, vir_index * width_b, width_b, 0)
    denominator = pair_energy[None, None, :] - eps_vir[:, None, None] - energy_cols[None, :, None]
    return (relaid.astype(jnp.float32) - mirrored.astype(jnp.float32)) / denominator


def solution(mesh):
    in_specs = (P("occ", None, "vir", None), P("vir", "occ", None), P(), P(), P())
    out_specs = P(None, "vir", "occ")
    return jax.shard_map(shards, mesh=mesh, in_specs=in_specs, out_specs=out_specs, check_vma=False)
```

profile of v0, /device:TPU:0, one launch (start us, length us, event | category | flops | bytes accessed | tf_op | source)
XLA Modules:
  0.0 1484.9 jit_solution(17963957135518208131)
XLA Ops:
  7.2 6.2 constant_dynamic-slice_fusion
  13.4 4.9 copy.27
  18.4 56.2 %all-gather.3.cloned.1.call-done = bf16[10,40,3200]{1,2,0:T(8,128)(2,1)} async-done(((bf16[10,40,400]{1,2,0:T(8,128)(2,1)}), bf16[10,40,3200]{1,2,0:T(8,128)(2,1)}) %all-gather.3.cloned.1.call-update) | async-done | bytes 2560016 | tf_op jit(solution)/shard_map/all_gather | solution.py:20
  74.6 8.3 copy.28
  82.9 33.5 %reshape.69 = bf16[5000,3200]{1,0:T(8,128)(2,1)} reshape(bf16[50,100,3200]{2,1,0:T(8,128)(2,1)} %param.6) | data formatting | bytes 64000000 | tf_op jit(solution)/shard_map/reshape | solution.py:18
  116.4 146.5 %all-gather.5.cloned.1.call-done = bf16[1600,3200]{1,0:T(8,128)(2,1)} async-done(((bf16[400,3200]{1,0:T(8,128)(2,1)}), bf16[1600,3200]{1,0:T(8,128)(2,1)}) %all-gather.5.cloned.1.call-update) | async-done | bytes 10240016 | tf_op jit(solution)/shard_map/all_gather | solution.py:24
  263.0 65.0 %multiply_bitcast_fusion = f32[5000,1600]{0,1:T(8,128)} fusion(bf16[1600,3200]{1,0:T(8,128)(2,1)} %all-gather.5.cloned.1.call-done, bf16[5000,3200]{1,0:T(8,128)(2,1)} %reshape.69), kind=kOutput, calls=%fused_computation.4 | convolution fusion | flops 51207999488 | bytes 74240000 | tf_op jit(solution)/shard_map/dot_general | solution.py:22
  327.9 43.7 %mul.29 = f32[50,100,40,40]{1,0,3,2:T(8,128)} reshape(f32[5000,1600]{0,1:T(8,128)} %multiply_bitcast_fusion) | data formatting | bytes 64000000 | tf_op jit(solution)/shard_map/mul | solution.py:28
  371.7 36.6 %fusion = bf16[50,100,40,40]{1,0,3,2:T(8,128)(2,1)} fusion(f32[50,100,40,40]{1,0,3,2:T(8,128)} %mul.29), kind=kLoop, calls=%fused_computation.1 | loop fusion | flops 16000000 | bytes 48000000 | tf_op jit(solution)/shard_map/convert_element_type | solution.py:29
  408.3 509.0 %all_to_all.27 = bf16[50,100,1600]{1,0,2:T(8,128)(2,1)} all-to-all(bf16[50,100,1600]{1,0,2:T(8,128)(2,1)} %bitcast.24), channel_id=1, replica_groups=mesh['occ'=4,'vir'=8] {'occ'}, dimensions={2} | all-to-all | bytes 32000000 | tf_op jit(solution)/shard_map/all_to_all | solution.py:31
  917.3 35.0 %copy.35 = bf16[50,100,4,400]{3,2,1,0:T(4,128)(2,1)} copy(bf16[50,100,4,400]{1,0,3,2:T(8,128)(2,1)} %bitcast.25) | data formatting | bytes 32000000 | tf_op jit(solution)/shard_map/all_to_all | solution.py:31
  952.3 20.3 %copy.31 = bf16[50,4,100,400]{3,2,1,0:T(8,128)(2,1)} copy(bf16[50,4,100,400]{3,1,2,0:T(4,128)(2,1)} %bitcast.26) | data formatting | bytes 32000000 | tf_op jit(solution)/shard_map/all_to_all | solution.py:31
  972.6 28.9 %all_to_all.23 = bf16[50,400,400]{2,1,0:T(8,128)(2,1)} reshape(bf16[50,4,100,400]{3,2,1,0:T(8,128)(2,1)} %copy.31) | data formatting | bytes 32000000 | tf_op jit(solution)/shard_map/all_to_all | solution.py:31
  1001.5 30.0 %copy.32 = bf16[50,400,400]{2,0,1:T(8,128)(2,1)} copy(bf16[50,400,400]{2,1,0:T(8,128)(2,1)} %all_to_all.23) | data formatting | bytes 32000000 | tf_op jit(solution)/shard_map/all_to_all | solution.py:31
  1031.4 6.4 all-to-all-start.1
  1038.0 0.1 add.34
  1038.1 0.1 dynamic_slice.11
  1038.2 0.1 broadcast_subtract_fusion
  1038.3 249.5 %all-to-all-done.1 = bf16[50,400,400]{2,0,1:T(8,128)(2,1)} async-done(((bf16[50,400,400]{2,0,1:T(8,128)(2,1)}), bf16[50,400,400]{2,0,1:T(8,128)(2,1)}, u32[]{:S(2)}, u32[]{:S(2)}) %all-to-all-start.1) | async-done | bytes 16000032 | tf_op jit(solution)/shard_map/all_to_all | solution.py:32
  1287.8 24.7 %copy_convert_fusion = f32[50,400,400]{2,1,0:T(8,128)} fusion(bf16[50,400,400]{2,0,1:T(8,128)(2,1)} %all-to-all-done.1), kind=kLoop, calls=%fused_computation.5 | loop fusion | flops 8000000 | bytes 48000000 | tf_op jit(solution)/shard_map/convert_element_type | solution.py:43
  1312.4 41.8 %reshape.72 = f32[50,8,50,400]{3,2,1,0:T(8,128)} reshape(f32[50,400,400]{2,1,0:T(8,128)} %copy_convert_fusion) | data formatting | bytes 64000000 | tf_op jit(solution)/shard_map/convert_element_type | solution.py:43
  1354.2 48.8 %copy.34 = f32[8,50,50,400]{3,1,0,2:T(8,128)} copy(f32[8,50,50,400]{3,2,0,1:T(8,128)} %bitcast.23) | data formatting | bytes 64000000 | tf_op jit(solution)/shard_map/convert_element_type | solution.py:43
  1403.0 41.8 %reshape.71 = f32[400,50,400]{2,0,1:T(8,128)} reshape(f32[8,50,50,400]{3,1,0,2:T(8,128)} %copy.34) | data formatting | bytes 64000000 | tf_op jit(solution)/shard_map/convert_element_type | solution.py:43
  1444.8 33.2 %fusion.1 = f32[400,50,400]{2,0,1:T(8,128)} fusion(f32[400,50,400]{2,0,1:T(8,128)} %reshape.71, bf16[50,400,400]{2,1,0:T(8,128)(2,1)} %all_to_all.23, f32[50]{0:T(128)S(1)} %dynamic_slice.11, f32[400,400]{1,0:T(8,128)S(1)} %broadcast_subtract_fusion), kind=kLoop, calls=%fused_computation.3 | loop fusion | flops 32000000 | bytes 80640200 | tf_op jit(solution)/shard_map/div | solution.py:43
  (10 shorter events, 0.2 us)
Async XLA Ops:
  6.5 68.1 %all-gather.3.cloned.1.call-start = ((), (), s32[]{:S(2)}) async-start(), calls=%async_computation.2 | async-start | bytes 9216000 | tf_op jit(solution)/shard_map/all_gather | solution.py:20
  18.3 244.6 %all-gather.5.cloned.1.call-start = ((), (), s32[]{:S(2)}) async-start(), calls=%async_computation.3 | async-start | bytes 12800000 | tf_op jit(solution)/shard_map/all_gather | solution.py:24
  1031.4 6.4 copy-start.1
  1031.4 6.6 copy-start
  1031.4 256.3 %all-to-all-start.1 = ((bf16[50,400,400]{2,0,1:T(8,128)(2,1)}), bf16[50,400,400]{2,0,1:T(8,128)(2,1)}, u32[]{:S(2)}, u32[]{:S(2)}) async-start(bf16[50,400,400]{2,0,1:T(8,128)(2,1)} %copy.32), calls=%async_computation.1 | async-start | bytes 45875200 | tf_op jit(solution)/shard_map/all_to_all | solution.py:32
Sparse Core Ops, SparseCore 0:
  18.5 56.1 all-gather.2
  83.1 179.8 all-gather.4
where the time goes:
time: 1490 us; the launch traced here: 1480 us
  blocking collectives  509 us (34%)
  waiting for transfers between devices  452 us (30%)
  local copies, waits for them, and re-layouts  343 us (23%)
  other arithmetic  94.7 us (6%)
  matrix products  65 us (4%)
    all_to_all x1, blocking collectives, shards(): lax.all_to_all(mixed, 'occ', split_axis=2, concat_axis=1, tiled=True)  509 us
    all_to_all x1, waiting for transfers between devices, shards(): lax.all_to_all(own_rows, 'vir', split_axis=1, concat_axis=0, tiled=True)  249 us
    all_gather x1, waiting for transfers between devices, shards(): lax.all_gather(columns, 'occ', axis=0, tiled=True)  147 us
    convert_element_type x3, local copies, waits for them, and re-layouts, shards(): relaid.astype(jnp.float32) - mirrored.astype(jnp.float32)  132 us
    all_to_all x4, local copies, waits for them, and re-layouts, shards(): lax.all_to_all(mixed, 'occ', split_axis=2, concat_axis=1, tiled=True)  114 us
    dot_general x1, matrix products, shards(): lax.dot_general(weights_flat, lax.all_gather(columns, 'occ', axis=0, tile...  65 us
    all_gather x1, waiting for transfers between devices, shards(): columns = lax.all_gather(sliced, 'vir', axis=2, tiled=True)  56.2 us
    mul x1, local copies, waits for them, and re-layouts, shards(): ladder = 0.5 * ladder.reshape(block_a, block_b, occ_all, occ_all)  43.7 us
  transfers between devices with their start and end apart: 3, of which 3 were waited for; matrix products, arithmetic and copies ran while one was open for 2% of the time, Pallas kernels for 0%

commit v1 on v0

--- a/solution.py
+++ b/solution.py
@@ -28,7 +28,18 @@
     ladder = 0.5 * ladder.reshape(block_a, block_b, occ_all, occ_all)
     mixed = (ladder - jnp.transpose(ladder, (0, 1, 3, 2))).astype(jnp.bfloat16)
     mixed = mixed.reshape(block_a, block_b, occ_all * occ_all)
-    own_rows = lax.all_to_all(mixed, "occ", split_axis=2, concat_axis=1, tiled=True)
+    ways, here = (lax.axis_size("occ"), lax.axis_index("occ"))
+    width = mixed.shape[2] // ways
+    shape = list(mixed.shape)
+    shape[2] = width
+    height = shape[1]
+    shape[1] = height * ways
+    own_rows = jnp.zeros(shape, mixed.dtype)
+    for mask in range(ways):
+        part = lax.dynamic_slice_in_dim(mixed, (here ^ mask) * width, width, axis=2)
+        if mask:
+            part = lax.ppermute(part, "occ", [(d, d ^ mask) for d in range(ways)])
+        own_rows = lax.dynamic_update_slice_in_dim(own_rows, part, (here ^ mask) * height, axis=1)
     relaid = lax.all_to_all(own_rows, "vir", split_axis=1, concat_axis=0, tiled=True)
     mirrored = jnp.swapaxes(own_rows, 0, 1)
     pair_count = relaid.shape[2]

time: 1490 us -> 1400 us (0.940)
  the two profiles are of different devices: /device:TPU:0 before, /device:TPU:8 now
where the time goes in v1:
time: 1400 us; the launch traced here: 1390 us
  waiting for transfers between devices  753 us (54%)
  local copies, waits for them, and re-layouts  456 us (33%)
  other arithmetic  94.7 us (7%)
  matrix products  65 us (5%)
  between operations  14.1 us (1%)
    ppermute x3, waiting for transfers between devices, shards(): part = lax.ppermute(part, 'occ', [(d, d ^ mask) for d in range(ways)])  305 us
    all_to_all x1, waiting for transfers between devices, shards(): lax.all_to_all(own_rows, 'vir', split_axis=1, concat_axis=0, tiled=True)  249 us
    dynamic_update_slice x5, local copies, waits for them, and re-layouts, shards(): lax.dynamic_update_slice_in_dim(own_rows, part, (here ^ mask) * height, a...  168 us
    all_gather x1, waiting for transfers between devices, shards(): lax.all_gather(columns, 'occ', axis=0, tiled=True)  144 us
    convert_element_type x3, local copies, waits for them, and re-layouts, shards(): relaid.astype(jnp.float32) - mirrored.astype(jnp.float32)  132 us
    dot_general x1, matrix products, shards(): lax.dot_general(weights_flat, lax.all_gather(columns, 'occ', axis=0, tile...  65 us
    all_gather x1, waiting for transfers between devices, shards(): columns = lax.all_gather(sliced, 'vir', axis=2, tiled=True)  54.7 us
    mul x1, local copies, waits for them, and re-layouts, shards(): ladder = 0.5 * ladder.reshape(block_a, block_b, occ_all, occ_all)  43.7 us
  transfers between devices with their start and end apart: 6, of which 6 were waited for; matrix products, arithmetic and copies ran while one was open for 12% of the time, Pallas kernels for 0%

profile of v1, /device:TPU:8, one launch (start us, length us, event | category | flops | bytes accessed | tf_op | source)
XLA Modules:
  0.0 1394.7 jit_solution(598452933471791661)
XLA Ops:
  18.4 54.7 %all-gather.3.cloned.1.call-done = bf16[10,40,3200]{1,2,0:T(8,128)(2,1)} async-done(((bf16[10,40,400]{1,2,0:T(8,128)(2,1)}), bf16[10,40,3200]{1,2,0:T(8,128)(2,1)}) %all-gather.3.cloned.1.call-update) | async-done | bytes 2560016 | tf_op jit(solution)/shard_map/all_gather | solution.py:20
  73.1 8.3 copy.38
  81.4 33.5 %reshape.69 = bf16[5000,3200]{1,0:T(8,128)(2,1)} reshape(bf16[50,100,3200]{2,1,0:T(8,128)(2,1)} %param.6) | data formatting | bytes 64000000 | tf_op jit(solution)/shard_map/reshape | solution.py:18
  114.9 143.6 %all-gather.5.cloned.1.call-done = bf16[1600,3200]{1,0:T(8,128)(2,1)} async-done(((bf16[400,3200]{1,0:T(8,128)(2,1)}), bf16[1600,3200]{1,0:T(8,128)(2,1)}) %all-gather.5.cloned.1.call-update) | async-done | bytes 10240016 | tf_op jit(solution)/shard_map/all_gather | solution.py:24
  258.5 65.0 %multiply_bitcast_fusion = f32[5000,1600]{0,1:T(8,128)} fusion(bf16[1600,3200]{1,0:T(8,128)(2,1)} %all-gather.5.cloned.1.call-done, bf16[5000,3200]{1,0:T(8,128)(2,1)} %reshape.69), kind=kOutput, calls=%fused_computation.4 | convolution fusion | flops 51207999488 | bytes 74240000 | tf_op jit(solution)/shard_map/dot_general | solution.py:22
  323.4 43.7 %mul.53 = f32[50,100,40,40]{1,0,3,2:T(8,128)} reshape(f32[5000,1600]{0,1:T(8,128)} %multiply_bitcast_fusion) | data formatting | bytes 64000000 | tf_op jit(solution)/shard_map/mul | solution.py:28
  367.1 36.6 %fusion = bf16[50,100,40,40]{1,0,3,2:T(8,128)(2,1)} fusion(f32[50,100,40,40]{1,0,3,2:T(8,128)} %mul.53), kind=kLoop, calls=%fused_computation.1 | loop fusion | flops 16000000 | bytes 48000000 | tf_op jit(solution)/shard_map/convert_element_type | solution.py:29
  403.8 12.3 copy.40
  428.6 8.1 copy.41
  443.8 34.7 %dynamic_update_slice.12 = bf16[50,400,400]{2,1,0:T(8,128)(2,1)} dynamic-update-slice(bf16[50,400,400]{2,1,0:T(8,128)(2,1)} %broadcast_in_dim.2, bf16[50,100,400]{2,1,0:T(8,128)(2,1)} %copy.41, s32[]{:T(128)} %constant.4.clone.1, s32[]{:T(128)S(6)} %select_n.35, s32[]{:T(128)} %constant.4.clone.1) | dynamic-update-slice | bytes 8000004 | tf_op jit(solution)/shard_map/dynamic_update_slice | solution.py:42
  478.5 167.5 %collective-permute-done = bf16[50,100,400]{1,2,0:T(8,128)(2,1)} collective-permute-done((bf16[50,100,400]{1,2,0:T(8,128)(2,1)}, bf16[50,100,400]{1,2,0:T(8,128)(2,1)}, u32[]{:S(2)}, u32[]{:S(2)}) %collective-permute-start) | collective-permute-done | bytes 4000032 | tf_op jit(solution)/shard_map/ppermute | solution.py:41
  654.2 34.7 %dynamic_update_slice.13 = bf16[50,400,400]{2,1,0:T(8,128)(2,1)} dynamic-update-slice(bf16[50,400,400]{2,1,0:T(8,128)(2,1)} %dynamic_update_slice.12, bf16[50,100,400]{2,1,0:T(8,128)(2,1)} %copy.42, s32[]{:T(128)} %constant.4.clone.1, s32[]{:T(128)S(6)} %select_n.37, s32[]{:T(128)} %constant.4.clone.1) | dynamic-update-slice | bytes 8000004 | tf_op jit(solution)/shard_map/dynamic_update_slice | solution.py:42
  688.9 69.4 %collective-permute-done.1 = bf16[50,100,400]{1,2,0:T(8,128)(2,1)} collective-permute-done((bf16[50,100,400]{1,2,0:T(8,128)(2,1)}, bf16[50,100,400]{1,2,0:T(8,128)(2,1)}, u32[]{:S(2)}, u32[]{:S(2)}) %collective-permute-start.1) | collective-permute-done | bytes 4000032 | tf_op jit(solution)/shard_map/ppermute | solution.py:41
  766.4 33.5 %dynamic_update_slice.14 = bf16[50,400,400]{2,1,0:T(8,128)(2,1)} dynamic-update-slice(bf16[50,400,400]{2,1,0:T(8,128)(2,1)} %dynamic_update_slice.13, bf16[50,100,400]{2,1,0:T(8,128)(2,1)} %copy.43, s32[]{:T(128)} %constant.4.clone.1, s32[]{:T(128)S(6)} %select_n.39, s32[]{:T(128)} %constant.4.clone.1) | dynamic-update-slice | bytes 8000004 | tf_op jit(solution)/shard_map/dynamic_update_slice | solution.py:42
  799.9 68.4 %collective-permute-done.2 = bf16[50,100,400]{1,2,0:T(8,128)(2,1)} collective-permute-done((bf16[50,100,400]{1,2,0:T(8,128)(2,1)}, bf16[50,100,400]{1,2,0:T(8,128)(2,1)}, u32[]{:S(2)}, u32[]{:S(2)}) %collective-permute-start.2) | collective-permute-done | bytes 4000032 | tf_op jit(solution)/shard_map/ppermute | solution.py:41
  868.4 8.1 copy.44
  876.5 34.6 %dynamic_update_slice.15 = bf16[50,400,400]{2,1,0:T(8,128)(2,1)} dynamic-update-slice(bf16[50,400,400]{2,1,0:T(8,128)(2,1)} %dynamic_update_slice.14, bf16[50,100,400]{2,1,0:T(8,128)(2,1)} %copy.44, s32[]{:T(128)} %constant.4.clone.1, s32[]{:T(128)S(6)} %select_n.41, s32[]{:T(128)} %constant.4.clone.1) | dynamic-update-slice | bytes 8000004 | tf_op jit(solution)/shard_map/dynamic_update_slice | solution.py:42
  911.2 30.0 %copy.45 = bf16[50,400,400]{2,0,1:T(8,128)(2,1)} copy(bf16[50,400,400]{2,1,0:T(8,128)(2,1)} %dynamic_update_slice.15) | data formatting | bytes 32000000 | tf_op jit(solution)/shard_map/dynamic_update_slice | solution.py:42
  948.0 249.5 %all-to-all-done = bf16[50,400,400]{2,0,1:T(8,128)(2,1)} async-done(((bf16[50,400,400]{2,0,1:T(8,128)(2,1)}), bf16[50,400,400]{2,0,1:T(8,128)(2,1)}, u32[]{:S(2)}, u32[]{:S(2)}) %all-to-all-start) | async-done | bytes 16000032 | tf_op jit(solution)/shard_map/all_to_all | solution.py:43
  1197.5 24.7 %copy_convert_fusion = f32[50,400,400]{2,1,0:T(8,128)} fusion(bf16[50,400,400]{2,0,1:T(8,128)(2,1)} %all-to-all-done), kind=kLoop, calls=%fused_computation.5 | loop fusion | flops 8000000 | bytes 48000000 | tf_op jit(solution)/shard_map/convert_element_type | solution.py:54
  1222.1 41.8 %reshape.72 = f32[50,8,50,400]{3,2,1,0:T(8,128)} reshape(f32[50,400,400]{2,1,0:T(8,128)} %copy_convert_fusion) | data formatting | bytes 64000000 | tf_op jit(solution)/shard_map/convert_element_type | solution.py:54
  1263.9 48.9 %copy.47 = f32[8,50,50,400]{3,1,0,2:T(8,128)} copy(f32[8,50,50,400]{3,2,0,1:T(8,128)} %bitcast.21) | data formatting | bytes 64000000 | tf_op jit(solution)/shard_map/convert_element_type | solution.py:54
  1312.8 41.8 %reshape.71 = f32[400,50,400]{2,0,1:T(8,128)} reshape(f32[8,50,50,400]{3,1,0,2:T(8,128)} %copy.47) | data formatting | bytes 64000000 | tf_op jit(solution)/shard_map/convert_element_type | solution.py:54
  1354.6 33.2 %fusion.1 = f32[400,50,400]{2,0,1:T(8,128)} fusion(f32[400,50,400]{2,0,1:T(8,128)} %reshape.71, bf16[50,400,400]{2,1,0:T(8,128)(2,1)} %dynamic_update_slice.15, f32[50]{0:T(128)S(1)} %dynamic_slice.27, f32[400,400]{1,0:T(8,128)S(1)} %broadcast_subtract_fusion), kind=kLoop, calls=%fused_computation.3 | loop fusion | flops 32000000 | bytes 80640200 | tf_op jit(solution)/shard_map/div | solution.py:54
  (23 shorter events, 53.9 us)
Async XLA Ops:
  6.5 66.6 %all-gather.3.cloned.1.call-start = ((), (), s32[]{:S(2)}) async-start(), calls=%async_computation.1 | async-start | bytes 9216000 | tf_op jit(solution)/shard_map/all_gather | solution.py:20
  18.4 240.1 %all-gather.5.cloned.1.call-start = ((), (), s32[]{:S(2)}) async-start(), calls=%async_computation.2 | async-start | bytes 12800000 | tf_op jit(solution)/shard_map/all_gather | solution.py:24
  423.6 222.4 %collective-permute-start = (bf16[50,100,400]{1,2,0:T(8,128)(2,1)}, bf16[50,100,400]{1,2,0:T(8,128)(2,1)}, u32[]{:S(2)}, u32[]{:S(2)}) collective-permute-start(bf16[50,100,400]{1,2,0:T(8,128)(2,1)} %get-tuple-element.7), channel_id=1, source_target_pairs={{0,8},{8,0},{16,24},{24,16},{1,9},{9,1},{17,25},{25,17},{2,10},{10... | collective-permute-start | bytes 12000008 | tf_op jit(solution)/shard_map/ppermute | solution.py:41
  427.1 331.2 %collective-permute-start.1 = (bf16[50,100,400]{1,2,0:T(8,128)(2,1)}, bf16[50,100,400]{1,2,0:T(8,128)(2,1)}, u32[]{:S(2)}, u32[]{:S(2)}) collective-permute-start(bf16[50,100,400]{1,2,0:T(8,128)(2,1)} %get-tuple-element.6), channel_id=1, source_target_pairs={{0,16},{8,24},{16,0},{24,8},{1,17},{9,25},{17,1},{25,9},{2,18},{10... | collective-permute-start | bytes 12000008 | tf_op jit(solution)/shard_map/ppermute | solution.py:41
  427.7 440.7 %collective-permute-start.2 = (bf16[50,100,400]{1,2,0:T(8,128)(2,1)}, bf16[50,100,400]{1,2,0:T(8,128)(2,1)}, u32[]{:S(2)}, u32[]{:S(2)}) collective-permute-start(bf16[50,100,400]{1,2,0:T(8,128)(2,1)} %get-tuple-element.5), channel_id=1, source_target_pairs={{0,24},{8,16},{16,8},{24,0},{1,25},{9,17},{17,9},{25,1},{2,26},{10... | collective-permute-start | bytes 12000008 | tf_op jit(solution)/shard_map/ppermute | solution.py:41
  941.1 6.4 copy-start.1
  941.1 6.7 copy-start
  941.1 256.3 %all-to-all-start = ((bf16[50,400,400]{2,0,1:T(8,128)(2,1)}), bf16[50,400,400]{2,0,1:T(8,128)(2,1)}, u32[]{:S(2)}, u32[]{:S(2)}) async-start(bf16[50,400,400]{2,0,1:T(8,128)(2,1)} %copy.45), calls=%async_computation | async-start | bytes 45875200 | tf_op jit(solution)/shard_map/all_to_all | solution.py:43
Sparse Core Ops, SparseCore 0:
  18.5 54.5 all-gather.2
  81.5 176.9 all-gather.4
